TPU v7x, 512 devices: a whole 4x8x8 slice. The times are simulated.
512 devices in a mesh: pts: 64 (over y, x, core), tm: 8 (over z).
Axes of the slice: x: 4, y: 8, z: 8, core: 2. Of those that a mesh axis runs over, the one named last changes fastest.
Arguments:
- starting_location_factors: float32 [32768, 128], P('pts'), may hold values from -5 to 5
- starting_temporal_factors: float32 [8192, 128], P('tm'), may hold values from -5 to 5
- imposed_tension_record: float32 [32768, 8192], P('pts', 'tm'), may hold values from -10 to 10
- viscous_rate_factor: float32 [32768], P('pts'), may hold values from 0.2 to 1
- norton_power_law: float32 [32768], P('pts'), may hold values from 1.2 to 2.2
- space_inverse: float32 [128, 128], replicated, may hold values from -2 to 2
- time_inverse: float32 [128, 128], replicated, may hold values from -2 to 2
Outputs:
- space_out: float32 [32768, 128], P('pts')
- time_out: float32 [8192, 128], P('tm')
- misfit: float32 [2], replicated
All inputs are finite; a program needn't handle non-finite values.
Results may differ from a plain program's by a relative error of at most 0.0005.
Values sent between devices are 32-bit elements; how exact they have to be, the bound alone decides.
A program may use at most 64 MiB of HBM per device.

v0:
```python
import math
import jax
import jax.numpy as jnp
from jax import lax
from jax.sharding import PartitionSpec as P

ITERS = 2
highest = lax.Precision.HIGHEST


def viscous_pass(
    starting_location_factors,
    starting_temporal_factors,
    imposed_tension_record,
    viscous_rate_factor,
    norton_power_law,
):
    rank_scale = 1.0 / math.sqrt(starting_location_factors.shape[1])
    recon_field = (
        jnp.dot(starting_location_factors, starting_temporal_factors.T, precision=highest)
        * rank_scale
    )
    stress = imposed_tension_record - recon_field
    flow_rate = (
        viscous_rate_factor[:, None]
        * stress
        * jnp.power(stress * stress + 1e-06, 0.5 * (norton_power_law[:, None] - 1.0))
    )
    return (stress, flow_rate)


def shards(
    starting_location_factors,
    starting_temporal_factors,
    imposed_tension_record,
    viscous_rate_factor,
    norton_power_law,
    space_inverse,
    time_inverse,
):
    pts_count = lax.axis_size("pts")
    instant_count = lax.axis_size("tm")
    point_total = starting_location_factors.shape[0] * pts_count
    instant_total = starting_temporal_factors.shape[0] * instant_count
    share_rows = starting_temporal_factors.shape[0] // pts_count
    residual_record = []
    for sweep in range(ITERS):
        stress, flow_rate = viscous_pass(
            starting_location_factors,
            starting_temporal_factors,
            imposed_tension_record,
            viscous_rate_factor,
            norton_power_law,
        )
        residual_energy = jnp.sum(stress * stress)
        time_part = lax.dot_general(
            flow_rate, starting_location_factors, (((0,), (0,)), ((), ())), precision=highest
        )
        time_sum = lax.psum(time_part, "pts")
        temporal_factors_before_rescale = jnp.dot(time_sum, time_inverse, precision=highest)
        own_start = lax.axis_index("pts") * share_rows
        own_block = lax.dynamic_slice_in_dim(
            temporal_factors_before_rescale, own_start, share_rows, 0
        )
        temporal_magnitude_quad = jnp.sum(own_block * own_block, axis=0)
        space_part = jnp.dot(flow_rate, starting_temporal_factors, precision=highest)
        space_sum = lax.psum(space_part, "tm")
        space_raw = jnp.dot(space_sum, space_inverse, precision=highest)
        space_sq = jnp.sum(space_raw * space_raw, axis=0)
        space_sq = lax.psum(space_sq, "pts")
        temporal_magnitude_quad = lax.psum(temporal_magnitude_quad, ("pts", "tm"))
        residual_energy = lax.psum(residual_energy, ("pts", "tm"))
        starting_location_factors = space_raw / jnp.sqrt(space_sq / point_total + 1e-06)
        updated_time_modes = temporal_factors_before_rescale / jnp.sqrt(
            temporal_magnitude_quad / instant_total + 1e-06
        )
        starting_temporal_factors = updated_time_modes
        residual_record.append(residual_energy / (point_total * instant_total))
    return (starting_location_factors, starting_temporal_factors, jnp.stack(residual_record))


def solution(mesh):
    return jax.shard_map(
        shards,
        mesh=mesh,
        in_specs=(P("pts", None), P("tm", None), P("pts", "tm"), P("pts"), P("pts"), P(), P()),
        out_specs=(P("pts", None), P("tm", None), P()),
        check_vma=False,
    )
```

profile of v0, /device:TPU:1, one launch (start us, length us, event | category | flops | bytes accessed | tf_op | source)
XLA Modules:
  0.0 881.4 jit_solution(14366667147604201860)
XLA Ops:
  7.2 0.0 copy-start
  7.2 0.0 all-reduce.8.cloned.1.call-start
  7.2 0.7 add_multiply_fusion
  8.0 0.3 copy-done
  8.2 0.0 copy-start.4
  8.2 0.0 copy-start.7
  8.2 4.5 multiply_reduce_fusion.1
  12.7 0.0 copy-start.3
  12.7 1.3 copy-done.3
  14.1 0.0 copy-done.4
  14.1 0.0 copy-done.7
  14.1 7.1 fusion
  21.2 0.0 copy-start.5
  21.2 0.0 all-reduce.8.cloned.1.call-update
  21.2 0.0 copy-start.6
  21.3 0.0 copy-start.1
  21.3 0.2 all-reduce.6.cloned.1.call-start
  21.5 7.3 fusion.1
  28.8 0.0 all-reduce.6.cloned.1.call-update
  28.8 0.0 all-reduce.12.cloned.1.call-start
  28.9 189.0 %all-reduce.8.cloned.1.call-done = f32[1024,128]{1,0:T(8,128)} async-done(((f32[1024,128]{1,0:T(8,128)}), f32[1024,128]{1,0:T(8,128)}) %all-reduce.8.cloned.1.call-update) | async-done | bytes 524304 | tf_op jit(solution)/shard_map/psum | solution.py:59
  217.9 0.0 copy-done.5
  217.9 1.6 fusion.20
  219.5 99.1 %psum.73 = f32[128]{0:T(128)S(1)} all-reduce(f32[128]{0:T(128)S(1)} %multiply_reduce_fusion.5), channel_id=1, replica_groups=mesh['pts'=64,'tm'=8] {'pts','tm'}, use_global_device_ids=true, to_apply=%region_5.0 | all-reduce | flops 128 | bytes 1024 | tf_op jit(solution)/shard_map/psum | solution.py:71
  318.6 0.0 all-reduce.6.cloned.1.call-done
  318.6 0.0 copy-done.6
  318.6 1.3 multiply_reduce_fusion.3
  319.9 125.1 %psum.71 = f32[128]{0:T(128)} all-reduce(f32[128]{0:T(128)S(1)} %get-tuple-element.6), channel_id=1, replica_groups=mesh['pts'=64,'tm'=8] {'pts'}, use_global_device_ids=true, to_apply=%region_2.0 | all-reduce | flops 128 | bytes 1024 | tf_op jit(solution)/shard_map/psum | solution.py:70
  445.0 0.7 add_sqrt_fusion.3
  445.7 0.0 copy-done.1
  445.7 2.8 multiply_reduce_fusion
  448.5 0.0 copy-start.2
  448.5 1.3 copy-done.2
  449.9 7.1 fusion.2
  457.0 0.0 all-reduce.12.cloned.1.call-update
  457.0 0.3 all-reduce.10.cloned.1.call-start
  457.3 7.3 fusion.3
  464.6 0.0 all-reduce.10.cloned.1.call-update
  464.6 180.4 %all-reduce.12.cloned.1.call-done = f32[1024,128]{1,0:T(8,128)} async-done(((f32[1024,128]{1,0:T(8,128)}), f32[1024,128]{1,0:T(8,128)}) %all-reduce.12.cloned.1.call-update) | async-done | bytes 524304 | tf_op jit(solution)/shard_map/psum | solution.py:59
  645.0 1.6 fusion.21
  646.6 99.2 %all-reduce = (f32[128]{0:T(128)S(1)}, f32[]{:T(128)}, f32[]{:T(128)}) all-reduce(f32[128]{0:T(128)S(1)} %multiply_reduce_fusion.4, f32[]{:T(128)} %get-tuple-element.10, f32[]{:T(128)} %get-tuple-element.12), channel_id=1, replica_groups=mesh['pts'=64,'tm'=8] {'pts','tm'}, use_global_device_ids=true, to_apply=%region_11.0 | all-reduce | flops 130 | bytes 1040 | tf_op jit(solution)/shard_map/psum | solution.py:71
  747.1 0.8 broadcast_divide_fusion
  748.0 0.0 all-reduce.10.cloned.1.call-done
  748.0 1.3 multiply_reduce_fusion.2
  749.3 124.2 %psum.75 = f32[128]{0:T(128)S(1)} all-reduce(f32[128]{0:T(128)S(1)} %get-tuple-element.8), channel_id=1, replica_groups=mesh['pts'=64,'tm'=8] {'pts'}, use_global_device_ids=true, to_apply=%region_8.0 | all-reduce | flops 128 | bytes 1024 | tf_op jit(solution)/shard_map/psum | solution.py:70
  873.5 0.6 pad_maximum_fusion
  874.1 0.7 broadcast_divide_fusion.4
  (5 shorter events, 0.1 us)
Async XLA Ops:
  7.2 1.1 copy-start
  7.2 210.7 %all-reduce.8.cloned.1.call-start = ((), (), s32[]{:S(2)}) async-start(), calls=%async_computation.1 | async-start | bytes 1048576 | tf_op jit(solution)/shard_map/psum | solution.py:59
  8.2 5.9 copy-start.4
  8.2 5.9 copy-start.7
  12.7 1.4 copy-start.3
  21.2 196.7 %copy-start.5 = (f32[128,128]{1,0:T(8,128)S(1)}, f32[128,128]{1,0:T(8,128)}, u32[]{:S(2)}) copy-start(f32[128,128]{1,0:T(8,128)} %param.13) | copy-start | bytes 196612
  21.2 297.4 %copy-start.6 = (f32[128,128]{1,0:T(8,128)S(1)}, f32[128,128]{1,0:T(8,128)}, u32[]{:S(2)}) copy-start(f32[128,128]{1,0:T(8,128)} %param.12) | copy-start | bytes 196612
  21.3 424.4 %copy-start.1 = (f32[512,1024]{1,0:T(8,128)S(1)}, f32[512,1024]{1,0:T(8,128)}, u32[]{:S(2)}) copy-start(f32[512,1024]{1,0:T(8,128)} %param.9) | copy-start | bytes 6291460
  21.3 297.3 %all-reduce.6.cloned.1.call-start = ((), (), s32[]{:S(2)}) async-start(), calls=%async_computation | async-start | bytes 524288 | tf_op jit(solution)/shard_map/psum | solution.py:67
  28.8 616.1 %all-reduce.12.cloned.1.call-start = ((), (), s32[]{:S(2)}) async-start(), calls=%async_computation.3 | async-start | bytes 1048576 | tf_op jit(solution)/shard_map/psum | solution.py:59
  448.5 1.4 copy-start.2
  457.0 290.9 %all-reduce.10.cloned.1.call-start = ((), (), s32[]{:S(2)}) async-start(), calls=%async_computation.2 | async-start | bytes 524288 | tf_op jit(solution)/shard_map/psum | solution.py:67
Sparse Core Ops, SparseCore 0:
  21.4 196.4 all-reduce.7
  220.8 73.5 all-reduce.5
  457.1 187.8 all-reduce.11
  647.8 73.5 all-reduce.9
where the time goes:
time: 882 us; the launch traced here: 881 us
  blocking collectives  448 us (51%)
  waiting for transfers between devices  369 us (42%)
  matrix products  42 us (5%)
  between operations  15.1 us (2%)
    psum x2, waiting for transfers between devices, shards(): time_sum = lax.psum(time_part, 'pts')  369 us
    psum x2, blocking collectives, shards(): space_sq = lax.psum(space_sq, 'pts')  249 us
    psum x2, blocking collectives, shards(): temporal_magnitude_quad = lax.psum(temporal_magnitude_quad, ('pts', 'tm'))  198 us
  transfers between devices with their start and end apart: 4, of which 2 were waited for; matrix products, arithmetic and copies ran while one was open for 2% of the time, Pallas kernels for 0%

commit v1 on v0

--- a/solution.py
+++ b/solution.py
@@ -56,7 +56,7 @@
         time_part = lax.dot_general(
             flow_rate, starting_location_factors, (((0,), (0,)), ((), ())), precision=highest
         )
-        time_sum = lax.psum(time_part, "pts")
+        time_sum = jnp.sum(lax.all_gather(time_part, "pts"), axis=0)
         temporal_factors_before_rescale = jnp.dot(time_sum, time_inverse, precision=highest)
         own_start = lax.axis_index("pts") * share_rows
         own_block = lax.dynamic_slice_in_dim(

time: 882 us -> 671 us (0.76)
  waiting for transfers between devices: 369 us -> 134 us
  other arithmetic: 3.62 us -> 26.6 us
    psum x2 -> x0, waiting for transfers between devices: 369 us -> none  [shards(): time_sum = lax.psum(time_part, 'pts')]
    psum x2, waiting for transfers between devices: 0.01 us -> 134 us  [shards(): space_sum = lax.psum(space_part, 'tm')]
    reduce_sum x0 -> x2, other arithmetic: none -> 23.6 us  [shards(): time_sum = jnp.sum(lax.all_gather(time_part, 'pts'), axis=0)]
    psum x2, blocking collectives: 249 us -> 260 us  [shards(): space_sq = lax.psum(space_sq, 'pts')]
  transfers between devices with their start and end apart: 4 -> 4, of which waited for: 2 -> 2; matrix products, arithmetic and copies ran while one was open for 2% -> 3% of each run, Pallas kernels for 0% -> 0%
where the time goes in v1:
time: 671 us; the launch traced here: 669 us
  blocking collectives  451 us (67%)
  waiting for transfers between devices  134 us (20%)
  matrix products  38.2 us (6%)
  other arithmetic  26.6 us (4%)
  between operations  16.9 us (3%)
    psum x2, blocking collectives, shards(): space_sq = lax.psum(space_sq, 'pts')  260 us
    psum x2, blocking collectives, shards(): temporal_magnitude_quad = lax.psum(temporal_magnitude_quad, ('pts', 'tm'))  191 us
    psum x2, waiting for transfers between devices, shards(): space_sum = lax.psum(space_part, 'tm')  134 us
    reduce_sum x2, other arithmetic, shards(): time_sum = jnp.sum(lax.all_gather(time_part, 'pts'), axis=0)  23.6 us
    dot_general x2, matrix products, shards(): lax.dot_general(flow_rate, starting_location_factors, (((0,), (0,)), ((),...  15.9 us
  transfers between devices with their start and end apart: 4, of which 2 were waited for; matrix products, arithmetic and copies ran while one was open for 3% of the time, Pallas kernels for 0%

profile of v1, /device:TPU:1, one launch (start us, length us, event | category | flops | bytes accessed | tf_op | source)
XLA Modules:
  0.0 669.5 jit_solution(386541039057482174)
XLA Ops:
  8.0 0.0 copy-start
  8.0 0.0 all-reduce.4.cloned.1.call-start
  8.1 0.7 add_multiply_fusion
  8.8 0.3 copy-done
  9.1 0.0 copy-start.7
  9.1 4.5 multiply_reduce_fusion.1
  13.6 0.0 copy-start.4
  13.6 0.0 copy-done.7
  13.6 5.6 fusion.1
  19.1 0.0 copy-start.6
  19.1 0.0 all-reduce.4.cloned.1.call-update
  19.2 0.2 all-gather.5.cloned.1.call-start
  19.4 0.0 copy-done.4
  19.4 7.1 %fusion = f32[1024,128]{1,0:T(8,128)} fusion(f32[512,128]{1,0:T(8,128)S(1)} %copy-done.4, f32[512,1024]{1,0:T(8,128)S(1)} %get-tuple-element.13, f32[512]{0:T(512)S(1)} %add_multiply_fusion, f32[512]{0:T(512)S(1)} %copy-done.7), kind=kOutput, calls=%fused_computation.6 | convolution fusion | flops 807403520 | bytes 2887680 | tf_op jit(solution)/shard_map/dot_general | solution.py:56
  26.5 0.0 all-gather.5.cloned.1.call-update
  26.6 0.0 all-reduce.6.cloned.1.call-start
  26.6 72.5 %all-reduce.4.cloned.1.call-done = f32[512,128]{1,0:T(8,128)} async-done(((f32[512,128]{1,0:T(8,128)}), f32[512,128]{1,0:T(8,128)}) %all-reduce.4.cloned.1.call-update) | async-done | bytes 262160 | tf_op jit(solution)/shard_map/psum | solution.py:67
  99.1 0.0 copy-done.6
  99.1 1.3 multiply_reduce_fusion.3
  100.5 130.0 %psum.57 = f32[128]{0:T(128)S(1)} all-reduce(f32[128]{0:T(128)S(1)} %get-tuple-element.6), channel_id=1, replica_groups=mesh['pts'=64,'tm'=8] {'pts'}, use_global_device_ids=true, to_apply=%region_2.0 | all-reduce | flops 128 | bytes 1024 | tf_op jit(solution)/shard_map/psum | solution.py:70
  230.4 0.0 all-gather.5.cloned.1.call-done
  230.4 0.0 copy-start.5
  230.4 0.0 copy-start.2
  230.5 11.9 %reduce_sum.73 = f32[1024,128]{1,0:T(8,128)S(1)} reduce(f32[64,1024,128]{2,1,0:T(8,128)} %bitcast.16, f32[]{:T(128)} %constant.12.clone.1), dimensions={0}, to_apply=%region_3.0 | reduce | flops 8257536 | bytes 34078724 | tf_op jit(solution)/shard_map/reduce_sum | solution.py:59
  242.3 0.0 copy-done.5
  242.3 0.6 fusion.20
  242.9 95.5 %psum.58 = f32[128]{0:T(128)S(1)} all-reduce(f32[128]{0:T(128)S(1)} %multiply_reduce_fusion.5), channel_id=1, replica_groups=mesh['pts'=64,'tm'=8] {'pts','tm'}, use_global_device_ids=true, to_apply=%region_5.0 | all-reduce | flops 128 | bytes 1024 | tf_op jit(solution)/shard_map/psum | solution.py:71
  338.4 0.0 copy-done.2
  338.4 2.9 multiply_reduce_fusion
  341.3 0.0 copy-start.3
  341.3 1.3 copy-done.3
  342.6 5.7 fusion.3
  348.3 0.0 all-reduce.6.cloned.1.call-update
  348.3 0.3 all-gather.7.cloned.1.call-start
  348.6 8.7 %fusion.2 = f32[1024,128]{1,0:T(8,128)} fusion(f32[512,1024]{1,0:T(8,128)} %copy-done.3, f32[512]{0:T(512)S(1)} %add_multiply_fusion, f32[512]{0:T(512)S(1)} %copy-done.7, f32[512,128]{1,0:T(8,128)S(1)} %get-tuple-element.7, f32[128]{0:T(128)S(1)} %add_sqrt_fusion.3), kind=kOutput, calls=%fused_computation.8 | convolution fusion | flops 807469056 | bytes 2888192 | tf_op jit(solution)/shard_map/dot_general | solution.py:56
  357.4 0.0 all-gather.7.cloned.1.call-update
  357.4 61.8 %all-reduce.6.cloned.1.call-done = f32[512,128]{1,0:T(8,128)} async-done(((f32[512,128]{1,0:T(8,128)}), f32[512,128]{1,0:T(8,128)}) %all-reduce.6.cloned.1.call-update) | async-done | bytes 262160 | tf_op jit(solution)/shard_map/psum | solution.py:67
  419.2 1.3 multiply_reduce_fusion.2
  420.5 130.1 %psum.60 = f32[128]{0:T(128)S(1)} all-reduce(f32[128]{0:T(128)S(1)} %get-tuple-element.8), channel_id=1, replica_groups=mesh['pts'=64,'tm'=8] {'pts'}, use_global_device_ids=true, to_apply=%region_8.0 | all-reduce | flops 128 | bytes 1024 | tf_op jit(solution)/shard_map/psum | solution.py:70
  550.6 0.7 broadcast_divide_fusion.4
  551.4 0.0 all-gather.7.cloned.1.call-done
  551.4 0.0 copy-start.1
  551.4 11.7 %reduce_sum.76 = f32[1024,128]{1,0:T(8,128)S(1)} reduce(f32[64,1024,128]{2,1,0:T(8,128)} %bitcast.17, f32[]{:T(128)} %constant.12.clone.1), dimensions={0}, to_apply=%region_9.0 | reduce | flops 8257536 | bytes 34078724 | tf_op jit(solution)/shard_map/reduce_sum | solution.py:59
  563.1 0.6 fusion.21
  563.7 95.6 %all-reduce = (f32[128]{0:T(128)S(1)}, f32[]{:T(128)}, f32[]{:T(128)}) all-reduce(f32[128]{0:T(128)S(1)} %multiply_reduce_fusion.4, f32[]{:T(128)} %get-tuple-element.10, f32[]{:T(128)} %get-tuple-element.12), channel_id=1, replica_groups=mesh['pts'=64,'tm'=8] {'pts','tm'}, use_global_device_ids=true, to_apply=%region_11.0 | all-reduce | flops 130 | bytes 1040 | tf_op jit(solution)/shard_map/psum | solution.py:71
  660.6 0.8 broadcast_divide_fusion
  661.5 0.6 pad_maximum_fusion
  662.1 0.0 copy-done.1
  (6 shorter events, 0.1 us)
Async XLA Ops:
  8.0 1.1 copy-start
  8.0 91.1 %all-reduce.4.cloned.1.call-start = ((), (), s32[]{:S(2)}) async-start(), calls=%async_computation | async-start | bytes 524288 | tf_op jit(solution)/shard_map/psum | solution.py:67
  9.1 4.5 copy-start.7
  13.6 5.8 copy-start.4
  19.1 80.0 %copy-start.6 = (f32[128,128]{1,0:T(8,128)S(1)}, f32[128,128]{1,0:T(8,128)}, u32[]{:S(2)}) copy-start(f32[128,128]{1,0:T(8,128)} %param.12) | copy-start | bytes 196612
  19.2 211.3 %all-gather.5.cloned.1.call-start = ((), (), s32[]{:S(2)}) async-start(), calls=%async_computation.2 | async-start | bytes 34078720 | tf_op jit(solution)/shard_map/all_gather | solution.py:59
  26.6 392.6 %all-reduce.6.cloned.1.call-start = ((), (), s32[]{:S(2)}) async-start(), calls=%async_computation.1 | async-start | bytes 524288 | tf_op jit(solution)/shard_map/psum | solution.py:67
  230.4 11.9 %copy-start.5 = (f32[128,128]{1,0:T(8,128)S(1)}, f32[128,128]{1,0:T(8,128)}, u32[]{:S(2)}) copy-start(f32[128,128]{1,0:T(8,128)} %param.13) | copy-start | bytes 196612
  230.4 107.9 %copy-start.2 = (f32[512,1024]{1,0:T(8,128)S(1)}, f32[512,1024]{1,0:T(8,128)}, u32[]{:S(2)}) copy-start(f32[512,1024]{1,0:T(8,128)} %param.9) | copy-start | bytes 6291460
  341.3 1.4 copy-start.3
  348.3 203.1 %all-gather.7.cloned.1.call-start = ((), (), s32[]{:S(2)}) async-start(), calls=%async_computation.3 | async-start | bytes 34078720 | tf_op jit(solution)/shard_map/all_gather | solution.py:59
  551.4 110.7 %copy-start.1 = (f32[1024,128]{1,0:T(8,128)S(1)}, f32[1024,128]{1,0:T(8,128)}, u32[]{:S(2)}) copy-start(f32[1024,128]{1,0:T(8,128)} %param.8) | copy-start | bytes 1572868
Sparse Core Ops, SparseCore 0:
  19.3 79.7 all-reduce.3
  348.4 70.6 all-reduce.5
Sparse Core Ops, SparseCore 1:
  26.6 153.9 all-gather.4
  357.5 144.9 all-gather.6

commit v2 on v0

--- a/solution.py
+++ b/solution.py
@@ -68,7 +68,7 @@
         space_raw = jnp.dot(space_sum, space_inverse, precision=highest)
         space_sq = jnp.sum(space_raw * space_raw, axis=0)
         space_sq = lax.psum(space_sq, "pts")
-        temporal_magnitude_quad = lax.psum(temporal_magnitude_quad, ("pts", "tm"))
+        temporal_magnitude_quad = lax.psum(lax.psum(temporal_magnitude_quad, "tm"), "pts")
         residual_energy = lax.psum(residual_energy, ("pts", "tm"))
         starting_location_factors = space_raw / jnp.sqrt(space_sq / point_total + 1e-06)
         updated_time_modes = temporal_factors_before_rescale / jnp.sqrt(

time: 882 us -> 838 us (0.950)
  blocking collectives: 448 us -> 384 us
  waiting for transfers between devices: 369 us -> 390 us
    psum x2 -> x1, blocking collectives: 249 us -> 129 us  [shards(): space_sq = lax.psum(space_sq, 'pts')]
    psum x2, waiting for transfers between devices: 0.01 us -> 120 us  [shards(): space_sum = lax.psum(space_part, 'tm')]
    psum x2, waiting for transfers between devices: 369 us -> 270 us  [shards(): time_sum = lax.psum(time_part, 'pts')]
    psum x2 -> x4, blocking collectives: 198 us -> 256 us  [the longest x1 129 us: shards(): lax.psum(lax.psum(temporal_magnitude_quad, 'tm'), 'pts')]
  transfers between devices with their start and end apart: 4 -> 4, of which waited for: 2 -> 4; matrix products, arithmetic and copies ran while one was open for 2% -> 2% of each run, Pallas kernels for 0% -> 0%
where the time goes in v2:
time: 838 us
  waiting for transfers between devices  390 us (47%)
  blocking collectives  384 us (46%)
  matrix products  42 us (5%)
  between operations  15.1 us (2%)
    psum x2, waiting for transfers between devices, shards(): time_sum = lax.psum(time_part, 'pts')  270 us
    psum x1, blocking collectives, shards(): lax.psum(lax.psum(temporal_magnitude_quad, 'tm'), 'pts')  129 us
    psum x1, blocking collectives, shards(): space_sq = lax.psum(space_sq, 'pts')  129 us
    psum x2, waiting for transfers between devices, shards(): space_sum = lax.psum(space_part, 'tm')  120 us
    psum x1, blocking collectives, shards(): residual_energy = lax.psum(residual_energy, ('pts', 'tm'))  97.4 us
    psum x2, blocking collectives, shards(): lax.psum(temporal_magnitude_quad, 'tm')  29.2 us
  transfers between devices with their start and end apart: 4, of which 4 were waited for; matrix products, arithmetic and copies ran while one was open for 2% of the time, Pallas kernels for 0%

profile of v2, /device:TPU:1, one launch (start us, length us, event | category | flops | bytes accessed | tf_op | source)
XLA Modules:
  0.0 837.6 jit_solution(599517991562146468)
XLA Ops:
  7.2 0.0 copy-start
  7.2 0.0 all-reduce.10.cloned.1.call-start
  7.2 0.7 add_multiply_fusion
  8.0 0.3 copy-done
  8.2 0.0 copy-start.4
  8.2 0.0 copy-start.7
  8.2 4.5 multiply_reduce_fusion.1
  12.7 0.0 copy-start.3
  12.7 1.3 copy-done.3
  14.1 0.0 copy-done.4
  14.1 0.0 copy-done.7
  14.1 7.1 fusion
  21.2 0.0 copy-start.5
  21.2 0.0 all-reduce.10.cloned.1.call-update
  21.2 0.0 copy-start.6
  21.3 0.0 copy-start.1
  21.3 0.2 all-reduce.8.cloned.1.call-start
  21.5 7.3 fusion.1
  28.8 0.0 all-reduce.8.cloned.1.call-update
  28.8 0.0 all-reduce.14.cloned.1.call-start
  28.9 189.0 %all-reduce.10.cloned.1.call-done = f32[1024,128]{1,0:T(8,128)} async-done(((f32[1024,128]{1,0:T(8,128)}), f32[1024,128]{1,0:T(8,128)}) %all-reduce.10.cloned.1.call-update) | async-done | bytes 524304 | tf_op jit(solution)/shard_map/psum | solution.py:59
  217.9 0.0 copy-done.5
  217.9 1.6 fusion.20
  219.5 14.8 %psum.87 = f32[128]{0:T(128)} all-reduce(f32[128]{0:T(128)S(1)} %multiply_reduce_fusion.5), channel_id=1, replica_groups=mesh['pts'=64,'tm'=8] {'tm'}, use_global_device_ids=true, to_apply=%region_5.0 | all-reduce | flops 128 | bytes 1024 | tf_op jit(solution)/shard_map/psum | solution.py:71
  234.4 59.7 %all-reduce.8.cloned.1.call-done = f32[512,128]{1,0:T(8,128)} async-done(((f32[512,128]{1,0:T(8,128)}), f32[512,128]{1,0:T(8,128)}) %all-reduce.8.cloned.1.call-update) | async-done | bytes 262160 | tf_op jit(solution)/shard_map/psum | solution.py:67
  294.0 0.0 copy-done.6
  294.0 1.3 multiply_reduce_fusion.3
  295.4 129.1 %all-reduce.2 = (f32[128]{0:T(128)S(1)}, f32[128]{0:T(128)S(1)}) all-reduce(f32[128]{0:T(128)} %psum.87, f32[128]{0:T(128)S(1)} %get-tuple-element.9), channel_id=1, replica_groups=mesh['pts'=64,'tm'=8] {'pts'}, use_global_device_ids=true, to_apply=%region_6.0 | all-reduce | flops 256 | bytes 2048 | tf_op jit(solution)/shard_map/psum | solution.py:71
  424.4 0.0 copy-done.1
  424.4 0.0 copy-start.8
  424.5 2.8 multiply_reduce_fusion
  427.3 0.0 copy-start.2
  427.3 1.3 copy-done.2
  428.6 0.0 copy-done.8
  428.6 7.1 fusion.2
  435.8 0.0 all-reduce.14.cloned.1.call-update
  435.8 0.0 all-reduce.12.cloned.1.call-start
  435.8 97.4 %all-reduce = (f32[]{:T(128)}, f32[]{:T(128)}) all-reduce(f32[]{:T(128)} %get-tuple-element.13, f32[]{:T(128)} %get-tuple-element.15), channel_id=1, replica_groups=mesh['pts'=64,'tm'=8] {'pts','tm'}, use_global_device_ids=true, to_apply=%region_17.0 | all-reduce | flops 2 | bytes 16 | tf_op jit(solution)/shard_map/psum | solution.py:72
  534.5 7.3 fusion.3
  541.8 0.0 all-reduce.12.cloned.1.call-update
  541.8 0.6 pad_maximum_fusion
  542.4 80.9 %all-reduce.14.cloned.1.call-done = f32[1024,128]{1,0:T(8,128)} async-done(((f32[1024,128]{1,0:T(8,128)}), f32[1024,128]{1,0:T(8,128)}) %all-reduce.14.cloned.1.call-update) | async-done | bytes 524304 | tf_op jit(solution)/shard_map/psum | solution.py:59
  623.3 1.6 fusion.21
  624.9 14.4 %psum.92 = f32[128]{0:T(128)S(1)} all-reduce(f32[128]{0:T(128)S(1)} %multiply_reduce_fusion.4), channel_id=1, replica_groups=mesh['pts'=64,'tm'=8] {'tm'}, use_global_device_ids=true, to_apply=%region_12.0 | all-reduce | flops 128 | bytes 1024 | tf_op jit(solution)/shard_map/psum | solution.py:71
  639.3 60.1 %all-reduce.12.cloned.1.call-done = f32[512,128]{1,0:T(8,128)} async-done(((f32[512,128]{1,0:T(8,128)}), f32[512,128]{1,0:T(8,128)}) %all-reduce.12.cloned.1.call-update) | async-done | bytes 262160 | tf_op jit(solution)/shard_map/psum | solution.py:67
  699.4 1.3 multiply_reduce_fusion.2
  700.7 128.7 %all-reduce.1 = (f32[128]{0:T(128)S(1)}, f32[128]{0:T(128)S(1)}) all-reduce(f32[128]{0:T(128)S(1)} %get-tuple-element.11, f32[128]{0:T(128)S(1)} %psum.92), channel_id=1, replica_groups=mesh['pts'=64,'tm'=8] {'pts'}, use_global_device_ids=true, to_apply=%region_9.0 | all-reduce | flops 256 | bytes 2048 | tf_op jit(solution)/shard_map/psum | solution.py:70
  829.4 0.8 broadcast_divide_fusion
  830.3 0.7 broadcast_divide_fusion.4
  (5 shorter events, 0.1 us)
Async XLA Ops:
  7.2 1.1 copy-start
  7.2 210.7 %all-reduce.10.cloned.1.call-start = ((), (), s32[]{:S(2)}) async-start(), calls=%async_computation.1 | async-start | bytes 1048576 | tf_op jit(solution)/shard_map/psum | solution.py:59
  8.2 5.9 copy-start.4
  8.2 5.9 copy-start.7
  12.7 1.4 copy-start.3
  21.2 196.7 %copy-start.5 = (f32[128,128]{1,0:T(8,128)S(1)}, f32[128,128]{1,0:T(8,128)}, u32[]{:S(2)}) copy-start(f32[128,128]{1,0:T(8,128)} %param.13) | copy-start | bytes 196612
  21.2 272.8 %copy-start.6 = (f32[128,128]{1,0:T(8,128)S(1)}, f32[128,128]{1,0:T(8,128)}, u32[]{:S(2)}) copy-start(f32[128,128]{1,0:T(8,128)} %param.12) | copy-start | bytes 196612
  21.3 403.2 %copy-start.1 = (f32[512,1024]{1,0:T(8,128)S(1)}, f32[512,1024]{1,0:T(8,128)}, u32[]{:S(2)}) copy-start(f32[512,1024]{1,0:T(8,128)} %param.9) | copy-start | bytes 6291460
  21.3 272.8 %all-reduce.8.cloned.1.call-start = ((), (), s32[]{:S(2)}) async-start(), calls=%async_computation | async-start | bytes 524288 | tf_op jit(solution)/shard_map/psum | solution.py:67
  28.8 594.5 %all-reduce.14.cloned.1.call-start = ((), (), s32[]{:S(2)}) async-start(), calls=%async_computation.3 | async-start | bytes 1048576 | tf_op jit(solution)/shard_map/psum | solution.py:59
  424.4 4.2 copy-start.8
  427.3 1.4 copy-start.2
  435.8 263.6 %all-reduce.12.cloned.1.call-start = ((), (), s32[]{:S(2)}) async-start(), calls=%async_computation.2 | async-start | bytes 524288 | tf_op jit(solution)/shard_map/psum | solution.py:67
Sparse Core Ops, SparseCore 0:
  21.4 196.4 all-reduce.9
  220.8 73.2 all-reduce.7
  435.9 187.3 all-reduce.13
  626.2 73.1 all-reduce.11
